TPU v7x, 256 devices: a whole 4x4x8 slice. The times are simulated.
256 devices in a mesh: ctx: 64 (over x, y_lo, z), rep: 4 (over y_hi, core).
Axes of the slice: x: 4, y: 4 (y_hi: 2, y_lo: 2; y = y_hi * 2 + y_lo), z: 8, core: 2. Of those that a mesh axis runs over, the one named last changes fastest.
Arguments:
- tokens: bfloat16 [4, 8192, 2880], P('rep', 'ctx'), may hold values from -6 to 6
- router_w: bfloat16 [2880, 32], replicated, may hold values from -0.109375 to 0.109375
- router_b: float32 [32], replicated, may hold values from -4 to 4
- hidden: bfloat16 [4, 8192, 4, 1536], P('rep', 'ctx'), may hold values from -6 to 6
- teacher_idx: int32 [4, 8192, 4], P('rep', 'ctx'), may hold values from 0 to 31, all different within a row
- merge_map: int32 [32], replicated, may hold values from 0 to 15, as said below
- merge_coef: float32 [32], replicated, may hold values from 0.3 to 1.5
- source_w: bfloat16 [32, 1536, 1536], P(None, 'ctx'), may hold values from -0.15625 to 0.15625
- out_grad: bfloat16 [4, 8192, 1536], P('rep', 'ctx'), may hold values from -6 to 6
Outputs:
- mixed: bfloat16 [4, 8192, 1536], P('rep', 'ctx')
- hidden_grad: bfloat16 [4, 8192, 4, 1536], P('rep', 'ctx')
- token_grad: bfloat16 [4, 8192, 2880], P('rep', 'ctx')
- router_w_grad: float32 [2880, 32], replicated
- router_b_grad: float32 [32], replicated
- coef_grad: float32 [32], replicated
- source_w_grad: float32 [32, 1536, 1536], P(None, 'ctx', 'rep')
Inputs may be any that keep to these rules, and one draw needn't show every extreme that they name: `teacher_idx`: each token names 4 different experts. `merge_map`: each of the 16 combinations takes exactly two of the 32 experts.
All inputs are finite; a program needn't handle non-finite values.
Results may differ from a plain program's by a relative error of at most 0.0064.
Values may be sent and summed in bfloat16 or wider, within the bound.
A program may use at most 128 MiB of HBM per device.

v0:
```python
import math
import jax
import jax.numpy as jnp
from jax import lax
from jax.sharding import PartitionSpec as P

MERGED = 16


def expert_rows(rows_hidden, rows_grad, rows_member, lane_weights):
    row_count = rows_hidden.shape[0]
    out_rows = jnp.zeros((row_count, lane_weights.shape[1]), jnp.float32)
    back_rows = jnp.zeros((row_count, lane_weights.shape[2]), jnp.float32)
    weight = lane_weights[0]
    selected = (rows_member == 0)[:, None]
    forward = lax.dot_general(
        rows_hidden, weight, (((1,), (1,)), ((), ())), preferred_element_type=jnp.float32
    )
    out_rows = jnp.where(selected, forward, out_rows)
    backward = jnp.dot(rows_grad, weight, preferred_element_type=jnp.float32)
    back_rows = jnp.where(selected, backward, back_rows)
    masked = jnp.where(selected, rows_grad, jnp.zeros_like(rows_grad))
    grad_list = [
        lax.dot_general(
            masked, rows_hidden, (((0,), (0,)), ((), ())), preferred_element_type=jnp.float32
        )
    ]
    return (out_rows, back_rows, jnp.stack(grad_list))


def on_device(
    tokens, router_w, router_b, hidden, teacher_idx, merge_map, merge_coef, source_w, out_grad
):
    ctx_count = lax.axis_size("ctx")
    rep_count = lax.axis_size("rep")
    tok_count = tokens.shape[1]
    feature_count = tokens.shape[2]
    top_count = teacher_idx.shape[2]
    hidden_width = hidden.shape[3]
    out_width = out_grad.shape[2]
    source_count = router_w.shape[1]
    row_share = source_w.shape[1]
    per_lane = max(1, MERGED // ctx_count)
    copies = max(1, ctx_count // MERGED)
    capacity = 5 * tok_count * top_count // (4 * ctx_count)
    slot_count = tok_count * top_count
    grad_scale = 1.0 / math.sqrt(tok_count * ctx_count * rep_count)
    flat_x = tokens.reshape(tok_count, feature_count)
    logits = jnp.dot(flat_x, router_w, preferred_element_type=jnp.float32) + router_b
    choice_ids = teacher_idx.reshape(tok_count, top_count)
    pick_table = choice_ids[:, :, None] == jnp.arange(source_count, dtype=jnp.int32)[None, None, :]
    pick_float = pick_table.astype(jnp.float32)
    chosen = jnp.sum(pick_float * logits[:, None, :], axis=2)
    raised = jnp.exp(chosen)
    gate_probs = raised / jnp.sum(raised, axis=1, keepdims=True)
    merged_id = jnp.sum(jnp.where(pick_table, merge_map[None, None, :], 0), axis=2)
    position = lax.axis_index("ctx") * tok_count + jnp.arange(tok_count, dtype=jnp.int32)
    lane_id = merged_id // per_lane * copies + (position % copies)[:, None]
    member_id = (merged_id % per_lane).reshape(-1)
    lane_flat = lane_id.reshape(-1)
    onehot = (lane_flat[:, None] == jnp.arange(ctx_count, dtype=jnp.int32)[None, :]).astype(
        jnp.int32
    )
    before = jnp.cumsum(onehot, axis=0) - onehot
    slot_rank = jnp.sum(before * onehot, axis=1)
    is_kept = slot_rank < capacity
    slot_index = jnp.where(is_kept, lane_flat * capacity + slot_rank, ctx_count * capacity)
    slot_source = (
        jnp.full((ctx_count * capacity + 1,), slot_count, jnp.int32)
        .at[slot_index]
        .set(jnp.arange(slot_count, dtype=jnp.int32))[: ctx_count * capacity]
    )
    slot_grad = (gate_probs[:, :, None] * out_grad.reshape(tok_count, 1, out_width)).astype(
        jnp.bfloat16
    )
    pad_hidden = jnp.concatenate(
        [hidden.reshape(slot_count, hidden_width), jnp.zeros((1, hidden_width), jnp.bfloat16)],
        axis=0,
    )
    pad_grad = jnp.concatenate(
        [slot_grad.reshape(slot_count, out_width), jnp.zeros((1, out_width), jnp.bfloat16)], axis=0
    )
    pad_member = jnp.concatenate([member_id, jnp.zeros((1,), jnp.int32)], axis=0)
    send_hidden = pad_hidden[slot_source].reshape(ctx_count, capacity, hidden_width)
    send_grad = pad_grad[slot_source].reshape(ctx_count, capacity, out_width)
    send_member = pad_member[slot_source].reshape(ctx_count, capacity)
    lane_group = lax.axis_index("ctx") // copies
    same_group = merge_map[:, None] == merge_map[None, :]
    earlier = jnp.arange(source_count)[:, None] > jnp.arange(source_count)[None, :]
    member_rank = jnp.sum((same_group & earlier).astype(jnp.int32), axis=1)
    source_order = (
        jnp.zeros((source_count,), jnp.int32)
        .at[2 * merge_map + member_rank]
        .set(jnp.arange(source_count, dtype=jnp.int32))
    )
    picked = source_w[source_order].reshape(
        MERGED // per_lane, 2 * per_lane, row_share, hidden_width
    )
    outgoing = jnp.repeat(picked, copies, axis=0)
    arrived = lax.all_to_all(outgoing, "ctx", split_axis=0, concat_axis=2, tiled=True)
    coef_table = merge_coef[source_order].reshape(MERGED // per_lane, per_lane, 2)
    pair_coef = lax.dynamic_index_in_dim(coef_table, lane_group, 0, keepdims=False)
    lane_weights = (
        pair_coef[:, 0, None, None] * arrived[:, 0].astype(jnp.float32)
        + pair_coef[:, 1, None, None] * arrived[:, 1].astype(jnp.float32)
    ).astype(jnp.bfloat16)
    recv_hidden, recv_grad, recv_member = (
        lax.all_to_all(send_hidden, "ctx", split_axis=0, concat_axis=0, tiled=True),
        lax.all_to_all(send_grad, "ctx", split_axis=0, concat_axis=0, tiled=True),
        lax.all_to_all(send_member, "ctx", split_axis=0, concat_axis=0, tiled=True),
    )
    out_rows, back_rows, lane_grads = expert_rows(
        recv_hidden.reshape(-1, hidden_width),
        recv_grad.reshape(-1, out_width),
        recv_member.reshape(-1),
        lane_weights,
    )
    home_out, home_back = (
        lax.all_to_all(
            out_rows.astype(jnp.bfloat16).reshape(ctx_count, capacity, out_width),
            "ctx",
            split_axis=0,
            concat_axis=0,
            tiled=True,
        ),
        lax.all_to_all(
            back_rows.astype(jnp.bfloat16).reshape(ctx_count, capacity, hidden_width),
            "ctx",
            split_axis=0,
            concat_axis=0,
            tiled=True,
        ),
    )
    slot_out = jnp.concatenate(
        [home_out.reshape(-1, out_width), jnp.zeros((1, out_width), jnp.bfloat16)], axis=0
    )[slot_index].reshape(tok_count, top_count, out_width)
    hidden_grad = jnp.concatenate(
        [home_back.reshape(-1, hidden_width), jnp.zeros((1, hidden_width), jnp.bfloat16)], axis=0
    )[slot_index].reshape(1, tok_count, top_count, hidden_width)
    mixed = (
        jnp.sum(gate_probs[:, :, None] * slot_out.astype(jnp.float32), axis=1)
        .astype(jnp.bfloat16)
        .reshape(1, tok_count, out_width)
    )
    score_grad = jnp.einsum(
        "td,tkd->tk",
        out_grad.reshape(tok_count, out_width),
        slot_out,
        preferred_element_type=jnp.float32,
    )
    chosen_grad = gate_probs * (
        score_grad - jnp.sum(gate_probs * score_grad, axis=1, keepdims=True)
    )
    logit_grad = jnp.sum(pick_float * chosen_grad[:, :, None], axis=1)
    logit_half = logit_grad.astype(jnp.bfloat16)
    token_grad = (
        lax.dot_general(
            logit_half, router_w, (((1,), (1,)), ((), ())), preferred_element_type=jnp.float32
        )
        .astype(jnp.bfloat16)
        .reshape(1, tok_count, feature_count)
    )
    part_router_w = lax.dot_general(
        flat_x, logit_half, (((0,), (0,)), ((), ())), preferred_element_type=jnp.float32
    )
    part_router_b = jnp.sum(logit_grad, axis=0)
    arrived_grads = lax.all_to_all(
        lane_grads.reshape(per_lane, ctx_count, row_share, hidden_width),
        "ctx",
        split_axis=1,
        concat_axis=0,
        tiled=True,
    )
    merged_grad = (
        arrived_grads.reshape(MERGED // per_lane, copies, per_lane, row_share, hidden_width)
        .sum(axis=1)
        .reshape(MERGED, row_share, hidden_width)
    )
    source_grad = merged_grad[merge_map]
    coef_part = jnp.einsum(
        "edf,edf->e", source_grad, source_w.astype(jnp.float32), precision=lax.Precision.HIGHEST
    )
    summed = lax.psum_scatter(
        source_grad * merge_coef[:, None, None], "rep", scatter_dimension=2, tiled=True
    )
    source_w_grad = summed * grad_scale
    router_sum, bias_sum, coef_sum = lax.psum(
        (part_router_w, part_router_b, coef_part), ("ctx", "rep")
    )
    return (
        mixed,
        hidden_grad,
        token_grad,
        router_sum * grad_scale,
        bias_sum * grad_scale,
        coef_sum * grad_scale,
        source_w_grad,
    )


def solution(mesh):
    in_specs = (
        P("rep", "ctx", None),
        P(),
        P(),
        P("rep", "ctx", None, None),
        P("rep", "ctx", None),
        P(),
        P(),
        P(None, "ctx", None),
        P("rep", "ctx", None),
    )
    out_specs = (
        P("rep", "ctx", None),
        P("rep", "ctx", None, None),
        P("rep", "ctx", None),
        P(),
        P(),
        P(),
        P(None, "ctx", "rep"),
    )
    return jax.shard_map(
        on_device, mesh=mesh, in_specs=in_specs, out_specs=out_specs, check_vma=False
    )
```

profile of v0, /device:TPU:1, one launch (start us, length us, event | category | flops | bytes accessed | tf_op | source)
XLA Modules:
  0.0 1014.5 jit_solution(12828136133311541424)
XLA Ops:
  17.5 13.5 %all-to-all-start = ((s32[64,1,10]{2,1,0:T(1,128)}), s32[64,1,10]{2,1,0:T(1,128)S(1)}, u32[]{:S(2)}, u32[]{:S(2)}) async-start(s32[64,1,10]{2,1,0:T(1,128)} %bitcast.5), calls=%async_computation | async-start | bytes 65536 | tf_op jit(solution)/shard_map/all_to_all | solution.py:110
  41.7 11.1 %all-to-all-start.1 = ((bf16[64,10,1536]{2,1,0:T(8,128)(2,1)}), bf16[64,10,1536]{2,1,0:T(8,128)(2,1)}, u32[]{:S(2)}, u32[]{:S(2)}) async-start(bf16[64,10,1536]{2,1,0:T(8,128)(2,1)} %reshape.274), calls=%async_computation.1 | async-start | bytes 6291456 | tf_op jit(solution)/shard_map/all_to_all | solution.py:108
  55.8 66.0 %all-to-all-done.1 = bf16[64,10,1536]{2,1,0:T(8,128)(2,1)} async-done(((bf16[64,10,1536]{2,1,0:T(8,128)(2,1)}), bf16[64,10,1536]{2,1,0:T(8,128)(2,1)}, u32[]{:S(2)}, u32[]{:S(2)}) %all-to-all-start.1) | async-done | bytes 1966112 | tf_op jit(solution)/shard_map/all_to_all | solution.py:108
  121.8 6.5 broadcast_in_dim.85
  128.3 10.5 %all-to-all-start.2 = ((bf16[64,2,24,1536]{3,2,1,0:T(8,128)(2,1)}), bf16[64,2,24,1536]{3,2,1,0:T(8,128)(2,1)}, u32[]{:S(2)}, u32[]{:S(2)}) async-start(bf16[64,2,24,1536]{3,2,1,0:T(8,128)(2,1)} %bitcast.77), calls=%async_computation.2 | async-start | bytes 18874368 | tf_op jit(solution)/shard_map/all_to_all | solution.py:100
  143.4 199.7 %all-to-all-done.2 = bf16[64,2,24,1536]{3,2,1,0:T(8,128)(2,1)} async-done(((bf16[64,2,24,1536]{3,2,1,0:T(8,128)(2,1)}), bf16[64,2,24,1536]{3,2,1,0:T(8,128)(2,1)}, u32[]{:S(2)}, u32[]{:S(2)}) %all-to-all-start.2) | async-done | bytes 9437216 | tf_op jit(solution)/shard_map/all_to_all | solution.py:100
  343.1 8.1 copy.44
  351.1 9.8 select_convert_fusion.1
  365.1 11.4 %all-to-all-start.3 = ((bf16[64,10,1536]{2,1,0:T(8,128)(2,1)}), bf16[64,10,1536]{2,1,0:T(8,128)(2,1)}, u32[]{:S(2)}, u32[]{:S(2)}) async-start(bf16[64,10,1536]{2,1,0:T(8,128)(2,1)} %reshape.279), calls=%async_computation.3 | async-start | bytes 6291456 | tf_op jit(solution)/shard_map/all_to_all | solution.py:119
  378.9 5.0 mul.171
  384.2 61.5 %all-to-all-done.3 = bf16[64,10,1536]{2,1,0:T(8,128)(2,1)} async-done(((bf16[64,10,1536]{2,1,0:T(8,128)(2,1)}), bf16[64,10,1536]{2,1,0:T(8,128)(2,1)}, u32[]{:S(2)}, u32[]{:S(2)}) %all-to-all-start.3) | async-done | bytes 1966112 | tf_op jit(solution)/shard_map/all_to_all | solution.py:119
  445.7 4.3 reshape.280
  469.9 11.0 %all-to-all-start.4 = ((bf16[64,10,1536]{2,1,0:T(8,128)(2,1)}), bf16[64,10,1536]{2,1,0:T(8,128)(2,1)}, u32[]{:S(2)}, u32[]{:S(2)}) async-start(bf16[64,10,1536]{2,1,0:T(8,128)(2,1)} %reshape.283), calls=%async_computation.4 | async-start | bytes 6291456 | tf_op jit(solution)/shard_map/all_to_all | solution.py:109
  485.1 64.7 %all-to-all-done.4 = bf16[64,10,1536]{2,1,0:T(8,128)(2,1)} async-done(((bf16[64,10,1536]{2,1,0:T(8,128)(2,1)}), bf16[64,10,1536]{2,1,0:T(8,128)(2,1)}, u32[]{:S(2)}, u32[]{:S(2)}) %all-to-all-start.4) | async-done | bytes 1966112 | tf_op jit(solution)/shard_map/all_to_all | solution.py:109
  558.4 9.7 convolution_bitcast_fusion
  568.1 10.7 %all-to-all-start.6 = ((f32[1,64,24,1536]{3,2,0,1:T(8,128)}), f32[1,64,24,1536]{3,2,0,1:T(8,128)}, u32[]{:S(2)}, u32[]{:S(2)}) async-start(f32[1,64,24,1536]{3,2,0,1:T(8,128)} %convolution_bitcast_fusion), calls=%async_computation.6 | async-start | bytes 18874368 | tf_op jit(solution)/shard_map/all_to_all | solution.py:167
  580.2 205.3 %all-to-all-done.6 = f32[1,64,24,1536]{3,2,0,1:T(8,128)} async-done(((f32[1,64,24,1536]{3,2,0,1:T(8,128)}), f32[1,64,24,1536]{3,2,0,1:T(8,128)}, u32[]{:S(2)}, u32[]{:S(2)}) %all-to-all-start.6) | async-done | bytes 9437216 | tf_op jit(solution)/shard_map/all_to_all | solution.py:167
  785.5 5.2 reduce_sum.102
  793.8 6.3 broadcast_multiply_fusion
  801.6 9.6 select_convert_fusion
  811.3 4.2 reshape.285
  815.5 12.3 %all-to-all-start.5 = ((bf16[64,10,1536]{2,1,0:T(8,128)(2,1)}), bf16[64,10,1536]{2,1,0:T(8,128)(2,1)}, u32[]{:S(2)}, u32[]{:S(2)}) async-start(bf16[64,10,1536]{2,1,0:T(8,128)(2,1)} %reshape.285), calls=%async_computation.5 | async-start | bytes 6291456 | tf_op jit(solution)/shard_map/all_to_all | solution.py:126
  832.1 81.9 %all-reduce.7.cloned.1.call-done = f32[2880,32]{0,1:T(8,128)} async-done(((f32[2880,32]{0,1:T(8,128)}), f32[2880,32]{0,1:T(8,128)}) %all-reduce.7.cloned.1.call-update) | async-done | bytes 368656 | tf_op jit(solution)/shard_map/psum | solution.py:187
  928.5 75.4 %all-reduce.4 = (f32[32]{0:T(128)S(1)}, f32[32]{0:T(128)S(1)}) all-reduce(f32[32]{0:T(128)S(1)} %get-tuple-element.7, f32[32]{0:T(128)S(1)} %get-tuple-element.16), channel_id=1, replica_groups=mesh['ctx'=64,'rep'=4] {'ctx','rep'}, use_global_device_ids=true, to_apply=%region_14.15 | all-reduce | flops 64 | bytes 512 | tf_op jit(solution)/shard_map/psum | solution.py:187
  (117 shorter events, 94.8 us)
Async XLA Ops:
  8.0 375.8 %copy-start = (bf16[1,128,2880]{1,2,0:T(8,128)(2,1)S(1)}, bf16[1,128,2880]{1,2,0:T(8,128)(2,1)}, u32[]{:S(2)}) copy-start(bf16[1,128,2880]{1,2,0:T(8,128)(2,1)} %param.9) | copy-start | bytes 2211844
  10.8 20.2 %copy-start.7 = (bf16[1,128,4,1536]{3,2,1,0:T(4,128)(2,1)S(1)}, bf16[1,128,4,1536]{3,2,1,0:T(4,128)(2,1)}, u32[]{:S(2)}) copy-start(bf16[1,128,4,1536]{3,2,1,0:T(4,128)(2,1)} %param.12) | copy-start | bytes 4718596
  17.5 24.2 %all-to-all-start = ((s32[64,1,10]{2,1,0:T(1,128)}), s32[64,1,10]{2,1,0:T(1,128)S(1)}, u32[]{:S(2)}, u32[]{:S(2)}) async-start(s32[64,1,10]{2,1,0:T(1,128)} %bitcast.5), calls=%async_computation | async-start | bytes 65536 | tf_op jit(solution)/shard_map/all_to_all | solution.py:110
  41.7 11.1 %copy-start.12 = (s32[32]{0:T(128)S(1)}, s32[32]{0:T(128)}, u32[]{:S(2)}) copy-start(s32[32]{0:T(128)} %param.14) | copy-start | bytes 388
  41.7 12.0 %copy-start.2 = (bf16[32,24,1536]{2,1,0:T(8,128)(2,1)S(1)}, bf16[32,24,1536]{2,1,0:T(8,128)(2,1)}, u32[]{:S(2)}) copy-start(bf16[32,24,1536]{2,1,0:T(8,128)(2,1)} %param.16) | copy-start | bytes 7077892
  41.7 80.1 %all-to-all-start.1 = ((bf16[64,10,1536]{2,1,0:T(8,128)(2,1)}), bf16[64,10,1536]{2,1,0:T(8,128)(2,1)}, u32[]{:S(2)}, u32[]{:S(2)}) async-start(bf16[64,10,1536]{2,1,0:T(8,128)(2,1)} %reshape.274), calls=%async_computation.1 | async-start | bytes 6291456 | tf_op jit(solution)/shard_map/all_to_all | solution.py:108
  128.3 10.5 %copy-start.1 = (f32[32]{0:T(128)S(1)}, f32[32]{0:T(128)}, u32[]{:S(2)}) copy-start(f32[32]{0:T(128)} %param.15) | copy-start | bytes 388
  128.3 214.8 %all-to-all-start.2 = ((bf16[64,2,24,1536]{3,2,1,0:T(8,128)(2,1)}), bf16[64,2,24,1536]{3,2,1,0:T(8,128)(2,1)}, u32[]{:S(2)}, u32[]{:S(2)}) async-start(bf16[64,2,24,1536]{3,2,1,0:T(8,128)(2,1)} %bitcast.77), calls=%async_computation.2 | async-start | bytes 18874368 | tf_op jit(solution)/shard_map/all_to_all | solution.py:100
  365.1 11.4 %copy-start.9 = (bf16[1,128,1536]{2,1,0:T(8,128)(2,1)S(1)}, bf16[1,128,1536]{2,1,0:T(8,128)(2,1)}, u32[]{:S(2)}) copy-start(bf16[1,128,1536]{2,1,0:T(8,128)(2,1)} %param.17) | copy-start | bytes 1179652
  365.1 80.5 %all-to-all-start.3 = ((bf16[64,10,1536]{2,1,0:T(8,128)(2,1)}), bf16[64,10,1536]{2,1,0:T(8,128)(2,1)}, u32[]{:S(2)}, u32[]{:S(2)}) async-start(bf16[64,10,1536]{2,1,0:T(8,128)(2,1)} %reshape.279), calls=%async_computation.3 | async-start | bytes 6291456 | tf_op jit(solution)/shard_map/all_to_all | solution.py:119
  378.9 5.0 copy-start.8
  378.9 5.0 copy-start.13
  378.9 5.2 copy-start.11
  454.6 3.0 copy-start.10
  457.5 1.8 copy-start.5
  469.9 80.0 %all-to-all-start.4 = ((bf16[64,10,1536]{2,1,0:T(8,128)(2,1)}), bf16[64,10,1536]{2,1,0:T(8,128)(2,1)}, u32[]{:S(2)}, u32[]{:S(2)}) async-start(bf16[64,10,1536]{2,1,0:T(8,128)(2,1)} %reshape.283), calls=%async_computation.4 | async-start | bytes 6291456 | tf_op jit(solution)/shard_map/all_to_all | solution.py:109
  552.7 5.7 copy-start.3
  568.1 217.4 %all-to-all-start.6 = ((f32[1,64,24,1536]{3,2,0,1:T(8,128)}), f32[1,64,24,1536]{3,2,0,1:T(8,128)}, u32[]{:S(2)}, u32[]{:S(2)}) async-start(f32[1,64,24,1536]{3,2,0,1:T(8,128)} %convolution_bitcast_fusion), calls=%async_computation.6 | async-start | bytes 18874368 | tf_op jit(solution)/shard_map/all_to_all | solution.py:167
  578.9 335.2 %all-reduce.7.cloned.1.call-start = ((), (), s32[]{:S(2)}) async-start(), calls=%async_computation.8 | async-start | bytes 753664 | tf_op jit(solution)/shard_map/psum | solution.py:187
  580.2 424.2 %reduce-scatter.2.cloned.1.call-start = ((), (), s32[]{:S(2)}) async-start(), calls=%async_computation.9 | async-start | bytes 5898240 | tf_op jit(solution)/shard_map/reduce_scatter | solution.py:183
  800.1 1.5 copy-start.4
  815.5 13.6 %copy-start.6 = (bf16[128,4,1536]{2,1,0:T(4,128)(2,1)S(1)}, bf16[128,4,1536]{2,1,0:T(4,128)(2,1)}, u32[]{:S(2)}) copy-start(bf16[128,4,1536]{2,1,0:T(4,128)(2,1)} %copy-done.5) | copy-start | bytes 4718596
  815.5 100.3 %all-to-all-start.5 = ((bf16[64,10,1536]{2,1,0:T(8,128)(2,1)}), bf16[64,10,1536]{2,1,0:T(8,128)(2,1)}, u32[]{:S(2)}, u32[]{:S(2)}) async-start(bf16[64,10,1536]{2,1,0:T(8,128)(2,1)} %reshape.285), calls=%async_computation.5 | async-start | bytes 6291456 | tf_op jit(solution)/shard_map/all_to_all | solution.py:126
Sparse Core Ops, SparseCore 0:
  585.8 328.2 all-reduce.6
Sparse Core Ops, SparseCore 1:
  800.2 83.5 reduce-scatter.1
where the time goes:
time: 1020 us; the launch traced here: 1010 us
  waiting for transfers between devices  679 us (67%)
  local copies, waits for them, and re-layouts  104 us (10%)
  starting transfers between devices  80.5 us (8%)
  blocking collectives  75.4 us (7%)
  matrix products  33.5 us (3%)
  other arithmetic  25.9 us (3%)
  between operations  16.1 us (2%)
    all_to_all x1, waiting for transfers between devices, on_device(): lax.all_to_all(lane_grads.reshape(per_lane, ctx_count, row_share, hidden_...  205 us
    all_to_all x1, waiting for transfers between devices, on_device(): lax.all_to_all(outgoing, 'ctx', split_axis=0, concat_axis=2, tiled=True)  200 us
    psum x1, waiting for transfers between devices, on_device(): lax.psum((part_router_w, part_router_b, coef_part), ('ctx', 'rep'))  81.9 us
    psum x1, blocking collectives, on_device(): lax.psum((part_router_w, part_router_b, coef_part), ('ctx', 'rep'))  75.4 us
    all_to_all x1, waiting for transfers between devices, on_device(): lax.all_to_all(send_hidden, 'ctx', split_axis=0, concat_axis=0, tiled=True)  66 us
    all_to_all x1, waiting for transfers between devices, on_device(): lax.all_to_all(send_grad, 'ctx', split_axis=0, concat_axis=0, tiled=True)  64.7 us
    all_to_all x1, waiting for transfers between devices, on_device(): lax.all_to_all(out_rows.astype(jnp.bfloat16).reshape(ctx_count, capacity,...  61.5 us
  transfers between devices with their start and end apart: 9, of which 6 were waited for; matrix products, arithmetic and copies ran while one was open for 8% of the time, Pallas kernels for 0%

commit v1 on v0

--- a/solution.py
+++ b/solution.py
@@ -185,7 +185,7 @@
     )
     source_w_grad = summed * grad_scale
     router_sum, bias_sum, coef_sum = lax.psum(
-        (part_router_w, part_router_b, coef_part), ("ctx", "rep")
+        lax.psum((part_router_w, part_router_b, coef_part), "rep"), "ctx"
     )
     return (
         mixed,

time: 1020 us -> 1430 us (1.40)
  the two profiles are of different devices: /device:TPU:1 before, /device:TPU:16 now
where the time goes in v1:
time: 1430 us; the launch traced here: 1420 us
  waiting for transfers between devices  1020 us (71%)
  blocking collectives  163 us (11%)
  local copies, waits for them, and re-layouts  104 us (7%)
  starting transfers between devices  60.6 us (4%)
  matrix products  33.5 us (2%)
  other arithmetic  25.9 us (2%)
  between operations  14.4 us (1%)
    psum x1, waiting for transfers between devices, on_device(): lax.psum(lax.psum((part_router_w, part_router_b, coef_part), 'rep'), 'ctx')  403 us
    all_to_all x1, waiting for transfers between devices, on_device(): lax.all_to_all(outgoing, 'ctx', split_axis=0, concat_axis=2, tiled=True)  202 us
    psum x1, blocking collectives, on_device(): lax.psum(lax.psum((part_router_w, part_router_b, coef_part), 'rep'), 'ctx')  155 us
    all_to_all x1, waiting for transfers between devices, on_device(): lax.all_to_all(lane_grads.reshape(per_lane, ctx_count, row_share, hidden_...  149 us
    all_to_all x1, waiting for transfers between devices, on_device(): lax.all_to_all(send_hidden, 'ctx', split_axis=0, concat_axis=0, tiled=True)  69.9 us
    all_to_all x1, waiting for transfers between devices, on_device(): lax.all_to_all(send_grad, 'ctx', split_axis=0, concat_axis=0, tiled=True)  69.8 us
    all_to_all x1, waiting for transfers between devices, on_device(): lax.all_to_all(out_rows.astype(jnp.bfloat16).reshape(ctx_count, capacity,...  66.8 us
    psum x1, waiting for transfers between devices, on_device(): lax.psum((part_router_w, part_router_b, coef_part), 'rep')  58.4 us
  transfers between devices with their start and end apart: 10, of which 7 were waited for; matrix products, arithmetic and copies ran while one was open for 6% of the time, Pallas kernels for 0%

profile of v1, /device:TPU:16, one launch (start us, length us, event | category | flops | bytes accessed | tf_op | source)
XLA Modules:
  0.0 1420.1 jit_solution(617011797049860384)
XLA Ops:
  16.6 12.7 all-to-all-start
  40.0 11.6 all-to-all-start.1
  54.7 69.9 %all-to-all-done.1 = bf16[64,10,1536]{2,1,0:T(8,128)(2,1)} async-done(((bf16[64,10,1536]{2,1,0:T(8,128)(2,1)}), bf16[64,10,1536]{2,1,0:T(8,128)(2,1)}, u32[]{:S(2)}, u32[]{:S(2)}) %all-to-all-start.1) | async-done | bytes 1966112 | tf_op jit(solution)/shard_map/all_to_all | solution.py:108
  124.6 6.5 broadcast_in_dim.85
  131.1 7.1 all-to-all-start.2
  142.8 202.0 %all-to-all-done.2 = bf16[64,2,24,1536]{3,2,1,0:T(8,128)(2,1)} async-done(((bf16[64,2,24,1536]{3,2,1,0:T(8,128)(2,1)}), bf16[64,2,24,1536]{3,2,1,0:T(8,128)(2,1)}, u32[]{:S(2)}, u32[]{:S(2)}) %all-to-all-start.2) | async-done | bytes 9437216 | tf_op jit(solution)/shard_map/all_to_all | solution.py:100
  344.8 8.1 copy.44
  352.9 9.8 select_convert_fusion.1
  366.9 7.9 all-to-all-start.3
  377.1 5.0 mul.171
  382.4 66.8 %all-to-all-done.3 = bf16[64,10,1536]{2,1,0:T(8,128)(2,1)} async-done(((bf16[64,10,1536]{2,1,0:T(8,128)(2,1)}), bf16[64,10,1536]{2,1,0:T(8,128)(2,1)}, u32[]{:S(2)}, u32[]{:S(2)}) %all-to-all-start.3) | async-done | bytes 1966112 | tf_op jit(solution)/shard_map/all_to_all | solution.py:119
  473.4 5.9 all-to-all-start.4
  483.5 69.8 %all-to-all-done.4 = bf16[64,10,1536]{2,1,0:T(8,128)(2,1)} async-done(((bf16[64,10,1536]{2,1,0:T(8,128)(2,1)}), bf16[64,10,1536]{2,1,0:T(8,128)(2,1)}, u32[]{:S(2)}, u32[]{:S(2)}) %all-to-all-start.4) | async-done | bytes 1966112 | tf_op jit(solution)/shard_map/all_to_all | solution.py:109
  562.0 9.7 convolution_bitcast_fusion
  571.6 5.9 all-to-all-start.6
  578.9 58.4 %all-reduce.9.cloned.1.call-done = f32[2880,32]{0,1:T(8,128)} async-done(((f32[2880,32]{0,1:T(8,128)}), f32[2880,32]{0,1:T(8,128)}) %all-reduce.9.cloned.1.call-update) | async-done | bytes 368656 | tf_op jit(solution)/shard_map/psum | solution.py:188
  637.3 149.4 %all-to-all-done.6 = f32[1,64,24,1536]{3,2,0,1:T(8,128)} async-done(((f32[1,64,24,1536]{3,2,0,1:T(8,128)}), f32[1,64,24,1536]{3,2,0,1:T(8,128)}, u32[]{:S(2)}, u32[]{:S(2)}) %all-to-all-start.6) | async-done | bytes 9437216 | tf_op jit(solution)/shard_map/all_to_all | solution.py:167
  786.7 5.2 reduce_sum.102
  795.0 6.3 broadcast_multiply_fusion
  802.8 9.7 select_convert_fusion
  816.7 9.4 all-to-all-start.5
  830.4 402.5 %all-reduce.11.cloned.1.call-done = f32[2880,32]{0,1:T(8,128)} async-done(((f32[2880,32]{0,1:T(8,128)}), f32[2880,32]{0,1:T(8,128)}) %all-reduce.11.cloned.1.call-update) | async-done | bytes 368656 | tf_op jit(solution)/shard_map/psum | solution.py:187
  1247.8 7.1 all-reduce.5
  1254.9 155.5 %all-reduce.4 = (f32[32]{0:T(128)S(1)}, f32[32]{0:T(128)S(1)}) all-reduce(f32[32]{0:T(128)S(1)} %get-tuple-element.11, f32[32]{0:T(128)S(1)} %get-tuple-element.12), channel_id=1, replica_groups=mesh['ctx'=64,'rep'=4] {'ctx'}, use_global_device_ids=true, to_apply=%region_16.17 | all-reduce | flops 64 | bytes 512 | tf_op jit(solution)/shard_map/psum | solution.py:187
  (121 shorter events, 103.7 us)
Async XLA Ops:
  7.2 374.9 %copy-start = (bf16[1,128,2880]{1,2,0:T(8,128)(2,1)S(1)}, bf16[1,128,2880]{1,2,0:T(8,128)(2,1)}, u32[]{:S(2)}) copy-start(bf16[1,128,2880]{1,2,0:T(8,128)(2,1)} %param.9) | copy-start | bytes 2211844
  10.0 19.4 %copy-start.7 = (bf16[1,128,4,1536]{3,2,1,0:T(4,128)(2,1)S(1)}, bf16[1,128,4,1536]{3,2,1,0:T(4,128)(2,1)}, u32[]{:S(2)}) copy-start(bf16[1,128,4,1536]{3,2,1,0:T(4,128)(2,1)} %param.12) | copy-start | bytes 4718596
  16.6 23.4 %all-to-all-start = ((s32[64,1,10]{2,1,0:T(1,128)}), s32[64,1,10]{2,1,0:T(1,128)S(1)}, u32[]{:S(2)}, u32[]{:S(2)}) async-start(s32[64,1,10]{2,1,0:T(1,128)} %bitcast.5), calls=%async_computation | async-start | bytes 65536 | tf_op jit(solution)/shard_map/all_to_all | solution.py:110
  40.0 11.6 copy-start.12
  40.0 12.6 copy-start.2
  40.0 84.6 %all-to-all-start.1 = ((bf16[64,10,1536]{2,1,0:T(8,128)(2,1)}), bf16[64,10,1536]{2,1,0:T(8,128)(2,1)}, u32[]{:S(2)}, u32[]{:S(2)}) async-start(bf16[64,10,1536]{2,1,0:T(8,128)(2,1)} %reshape.274), calls=%async_computation.1 | async-start | bytes 6291456 | tf_op jit(solution)/shard_map/all_to_all | solution.py:108
  131.1 7.1 copy-start.1
  131.1 213.7 %all-to-all-start.2 = ((bf16[64,2,24,1536]{3,2,1,0:T(8,128)(2,1)}), bf16[64,2,24,1536]{3,2,1,0:T(8,128)(2,1)}, u32[]{:S(2)}, u32[]{:S(2)}) async-start(bf16[64,2,24,1536]{3,2,1,0:T(8,128)(2,1)} %bitcast.77), calls=%async_computation.2 | async-start | bytes 18874368 | tf_op jit(solution)/shard_map/all_to_all | solution.py:100
  366.9 8.0 copy-start.9
  366.9 82.3 %all-to-all-start.3 = ((bf16[64,10,1536]{2,1,0:T(8,128)(2,1)}), bf16[64,10,1536]{2,1,0:T(8,128)(2,1)}, u32[]{:S(2)}, u32[]{:S(2)}) async-start(bf16[64,10,1536]{2,1,0:T(8,128)(2,1)} %reshape.279), calls=%async_computation.3 | async-start | bytes 6291456 | tf_op jit(solution)/shard_map/all_to_all | solution.py:119
  377.1 5.0 copy-start.8
  377.1 5.0 copy-start.13
  377.1 5.2 copy-start.11
  458.1 3.0 copy-start.10
  461.0 1.8 copy-start.5
  473.4 80.0 %all-to-all-start.4 = ((bf16[64,10,1536]{2,1,0:T(8,128)(2,1)}), bf16[64,10,1536]{2,1,0:T(8,128)(2,1)}, u32[]{:S(2)}, u32[]{:S(2)}) async-start(bf16[64,10,1536]{2,1,0:T(8,128)(2,1)} %reshape.283), calls=%async_computation.4 | async-start | bytes 6291456 | tf_op jit(solution)/shard_map/all_to_all | solution.py:109
  556.3 5.7 copy-start.3
  571.6 215.1 %all-to-all-start.6 = ((f32[1,64,24,1536]{3,2,0,1:T(8,128)}), f32[1,64,24,1536]{3,2,0,1:T(8,128)}, u32[]{:S(2)}, u32[]{:S(2)}) async-start(f32[1,64,24,1536]{3,2,0,1:T(8,128)} %convolution_bitcast_fusion), calls=%async_computation.6 | async-start | bytes 18874368 | tf_op jit(solution)/shard_map/all_to_all | solution.py:167
  577.5 59.8 %all-reduce.9.cloned.1.call-start = ((), (), s32[]{:S(2)}) async-start(), calls=%async_computation.8 | async-start | bytes 753664 | tf_op jit(solution)/shard_map/psum | solution.py:188
  578.8 654.2 %all-reduce.11.cloned.1.call-start = ((), (), s32[]{:S(2)}) async-start(), calls=%async_computation.9 | async-start | bytes 753664 | tf_op jit(solution)/shard_map/psum | solution.py:187
  637.3 773.7 %reduce-scatter.2.cloned.1.call-start = ((), (), s32[]{:S(2)}) async-start(), calls=%async_computation.10 | async-start | bytes 5898240 | tf_op jit(solution)/shard_map/reduce_scatter | solution.py:183
  801.3 1.5 copy-start.4
  816.7 10.7 copy-start.6
  816.7 418.0 %all-to-all-start.5 = ((bf16[64,10,1536]{2,1,0:T(8,128)(2,1)}), bf16[64,10,1536]{2,1,0:T(8,128)(2,1)}, u32[]{:S(2)}, u32[]{:S(2)}) async-start(bf16[64,10,1536]{2,1,0:T(8,128)(2,1)} %reshape.285), calls=%async_computation.5 | async-start | bytes 6291456 | tf_op jit(solution)/shard_map/all_to_all | solution.py:126
Sparse Core Ops, SparseCore 0:
  581.5 55.6 all-reduce.8
  639.9 593.0 all-reduce.10
  1235.8 53.1 reduce-scatter.1
